TPU v7x, 32 devices: a whole 2x2x4 slice. The times are simulated.
32 devices in a mesh: dp: 8 (over z, core), fsdp: 4 (over y, x).
Axes of the slice: x: 2, y: 2, z: 4, core: 2. Of those that a mesh axis runs over, the one named last changes fastest.
Arguments:
- inputs: bfloat16 [64, 512, 768], P(('dp', 'fsdp')), may hold values from -6 to 6
- segment_ids: int32 [64, 512], P(('dp', 'fsdp')), may hold values from 0 to 3, never falling along the last dimension, each value on 1 to 256 neighbouring positions
- cotangent: bfloat16 [64, 512, 768], P(('dp', 'fsdp')), may hold values from -9 to 9
- qkv_weight: bfloat16 [768, 2304], P(('dp', 'fsdp')), may hold values from -0.21875 to 0.21875
- out_weight: bfloat16 [768, 768], P(('dp', 'fsdp')), may hold values from -1.75 to 1.75
- up_weight: bfloat16 [768, 3072], P(('dp', 'fsdp')), may hold values from -0.21875 to 0.21875
- down_weight: bfloat16 [3072, 768], P(('dp', 'fsdp')), may hold values from -0.109375 to 0.109375
- query_bias_vector: bfloat16 [768], P(('dp', 'fsdp')), may hold values from -1.5 to 1.5
- value_bias_vector: bfloat16 [768], P(('dp', 'fsdp')), may hold values from -1.5 to 1.5
- out_bias: bfloat16 [768], P(('dp', 'fsdp')), may hold values from -1.5 to 1.5
- gain_one: bfloat16 [768], P(('dp', 'fsdp')), may hold values from 0.5 to 1.5
- shift_one: bfloat16 [768], P(('dp', 'fsdp')), may hold values from -1.5 to 1.5
- up_bias: bfloat16 [3072], P(('dp', 'fsdp')), may hold values from -1.5 to 1.5
- down_bias: bfloat16 [768], P(('dp', 'fsdp')), may hold values from -1.5 to 1.5
- gain_two: bfloat16 [768], P(('dp', 'fsdp')), may hold values from 0.5 to 1.5
- shift_two: bfloat16 [768], P(('dp', 'fsdp')), may hold values from -1.5 to 1.5
- query_down: bfloat16 [768, 8], replicated, may hold values from -0.21875 to 0.21875
- query_up_weight: bfloat16 [8, 768], replicated, may hold values from -2 to 2
- value_down: bfloat16 [768, 8], replicated, may hold values from -0.21875 to 0.21875
- value_up_weight: bfloat16 [8, 768], replicated, may hold values from -2 to 2
Outputs:
- output: bfloat16 [64, 512, 768], P(('dp', 'fsdp'))
- grad_input: float32 [64, 512, 768], P(('dp', 'fsdp'))
- grad_query_down: float32 [768, 8], replicated
- grad_query_up: float32 [8, 768], replicated
- grad_value_down: float32 [768, 8], replicated
- grad_value_up: float32 [8, 768], replicated
Inputs may be any that keep to these rules, and one draw needn't show every extreme that they name: `segment_ids`: within a pack the ids never fall; each of the 4 documents has 1 to 256 rows, and one has exactly 256.
All inputs are finite; a program needn't handle non-finite values.
Results may differ from a plain program's by a relative error of at most 0.015.
The roundings to bfloat16 on the way count: a program that leaves them out, or rounds other values in their place, can miss the bound.
Values may be sent and summed in bfloat16 or wider, within the bound.
No kernel may reach another device: no remote copies, remote signals or barrier semaphores. Data moves between devices by JAX's collectives and lax.ppermute only.
A program may use at most 128 MiB of HBM per device.

v0:
```python
from functools import partial
import jax
import jax.numpy as jnp
from jax import lax
from jax.sharding import PartitionSpec as P

HEADS = 12
HEAD_DIM = 64
highest_precision_mode = lax.Precision.HIGHEST
norm_epsilon = 1e-05
adapter_scale = 2.0


def layer_norm(value_rows, gain, shift):
    centred = value_rows - jnp.mean(value_rows, axis=-1, keepdims=True)
    variance = jnp.mean(centred * centred, axis=-1, keepdims=True)
    return centred * lax.rsqrt(variance + norm_epsilon) * gain + shift


def gelu_exact(value_rows):
    return jax.nn.gelu(value_rows, approximate=False)


def fetch_forward(qkv_weight, out_weight, up_weight, down_weight, vectors, up_bias):
    return (
        lax.all_gather(qkv_weight, ("dp", "fsdp"), axis=0, tiled=True),
        lax.all_gather(out_weight, ("dp", "fsdp"), axis=0, tiled=True),
        lax.all_gather(up_weight, ("dp", "fsdp"), axis=0, tiled=True),
        lax.all_gather(down_weight, ("dp", "fsdp"), axis=0, tiled=True),
        lax.all_gather(vectors, ("dp", "fsdp"), axis=1, tiled=True),
        lax.all_gather(up_bias, ("dp", "fsdp"), axis=0, tiled=True),
    )


def fetch_backward(qkv_weight, out_weight, up_weight, down_weight, gains):
    return (
        lax.all_gather(qkv_weight, ("dp", "fsdp"), axis=0, tiled=True),
        lax.all_gather(out_weight, ("dp", "fsdp"), axis=0, tiled=True),
        lax.all_gather(up_weight, ("dp", "fsdp"), axis=0, tiled=True),
        lax.all_gather(down_weight, ("dp", "fsdp"), axis=0, tiled=True),
        lax.all_gather(gains, ("dp", "fsdp"), axis=1, tiled=True),
    )


def segment_mask(segment):
    return (segment[:, None] == segment[None, :])[None]


def attend_pack(packed):
    query_rows, key_rows, value_rows, segment = packed
    scale = query_rows.shape[-1] ** (-0.5)
    raw_scores = jnp.einsum(
        "qhd,khd->hqk", query_rows, key_rows, preferred_element_type=jnp.float32
    )
    in_segment = segment_mask(segment)
    masked = jnp.where(in_segment, raw_scores * scale, -jnp.inf)
    highest = jnp.max(masked, axis=-1, keepdims=True)
    exponent = jnp.where(in_segment, jnp.exp(masked - highest), 0.0)
    row_total = jnp.sum(exponent, axis=-1, keepdims=True)
    probs_low = (exponent / row_total).astype(jnp.bfloat16)
    attended = jnp.einsum("hqk,khd->qhd", probs_low, value_rows, preferred_element_type=jnp.float32)
    return (attended, (highest + jnp.log(row_total))[..., 0])


def attend_back(packed):
    query_rows, key_rows, value_rows, segment, log_total, grad_mixed = packed
    scale = query_rows.shape[-1] ** (-0.5)
    raw_scores = jnp.einsum(
        "qhd,khd->hqk", query_rows, key_rows, preferred_element_type=jnp.float32
    )
    in_segment = segment_mask(segment)
    probs = jnp.where(in_segment, jnp.exp(raw_scores * scale - log_total[..., None]), 0.0)
    value_rows_gradient = jnp.einsum(
        "hqk,qhd->khd", probs.astype(jnp.bfloat16), grad_mixed, preferred_element_type=jnp.float32
    )
    grad_probs = jnp.einsum(
        "qhd,khd->hqk", grad_mixed, value_rows, preferred_element_type=jnp.float32
    )
    inner_sum = jnp.sum(probs * grad_probs, axis=-1, keepdims=True)
    grad_raw = (probs * (grad_probs - inner_sum) * scale).astype(jnp.bfloat16)
    query_rows_gradient = jnp.einsum(
        "hqk,khd->qhd", grad_raw, key_rows, preferred_element_type=jnp.float32
    )
    grad_keys = jnp.einsum("hqk,qhd->khd", grad_raw, query_rows, preferred_element_type=jnp.float32)
    return (
        query_rows_gradient.astype(jnp.bfloat16),
        grad_keys.astype(jnp.bfloat16),
        value_rows_gradient.astype(jnp.bfloat16),
    )


def local(
    inputs,
    segment_ids,
    cotangent,
    qkv_weight,
    out_weight,
    up_weight,
    down_weight,
    query_bias_vector,
    value_bias_vector,
    out_bias,
    gain_one,
    shift_one,
    up_bias,
    down_bias,
    gain_two,
    shift_two,
    query_down,
    query_up_weight,
    value_down,
    value_up_weight,
):
    vector_shards = jnp.stack(
        [
            query_bias_vector,
            value_bias_vector,
            out_bias,
            gain_one,
            shift_one,
            down_bias,
            gain_two,
            shift_two,
        ]
    )
    qkv_full, out_full, up_full, down_full, vector_full, up_bias_full = fetch_forward(
        qkv_weight, out_weight, up_weight, down_weight, vector_shards, up_bias
    )
    vectors = vector_full.astype(jnp.float32)
    packs, seq_len, width = inputs.shape
    rows = packs * seq_len
    flat_in = inputs.reshape(rows, width)
    flat_float = flat_in.astype(jnp.float32)
    projected_rows = jnp.dot(flat_in, qkv_full, preferred_element_type=jnp.float32)
    query_rank_rows = jnp.dot(flat_in, query_down, preferred_element_type=jnp.float32)
    value_rank_rows = jnp.dot(flat_in, value_down, preferred_element_type=jnp.float32)
    query_up_weight_float = query_up_weight.astype(jnp.float32)
    value_up_weight_float = value_up_weight.astype(jnp.float32)
    query_rows = (
        projected_rows[:, :width]
        + vectors[0]
        + adapter_scale
        * jnp.dot(query_rank_rows, query_up_weight_float, precision=highest_precision_mode)
    ).astype(jnp.bfloat16)
    key_rows = projected_rows[:, width : 2 * width].astype(jnp.bfloat16)
    value_rows = (
        projected_rows[:, 2 * width :]
        + vectors[1]
        + adapter_scale
        * jnp.dot(value_rank_rows, value_up_weight_float, precision=highest_precision_mode)
    ).astype(jnp.bfloat16)
    head_shape = (packs, seq_len, HEADS, HEAD_DIM)
    queries_heads = query_rows.reshape(head_shape)
    keys_heads = key_rows.reshape(head_shape)
    values_heads = value_rows.reshape(head_shape)
    attended, log_total = lax.map(
        attend_pack, (queries_heads, keys_heads, values_heads, segment_ids)
    )
    attended_low = attended.reshape(rows, width).astype(jnp.bfloat16)
    hidden_one = (
        flat_float
        + jnp.dot(attended_low, out_full, preferred_element_type=jnp.float32)
        + vectors[2]
    )
    normed_one = layer_norm(hidden_one, vectors[3], vectors[4])
    upper = jnp.dot(
        normed_one.astype(jnp.bfloat16), up_full, preferred_element_type=jnp.float32
    ) + up_bias_full.astype(jnp.float32)
    activated, gelu_pull = jax.vjp(gelu_exact, upper)
    hidden_two = (
        normed_one
        + jnp.dot(activated.astype(jnp.bfloat16), down_full, preferred_element_type=jnp.float32)
        + vectors[5]
    )
    output = layer_norm(hidden_two, vectors[6], vectors[7]).astype(jnp.bfloat16)
    gain_shards = jnp.stack([gain_one, gain_two])
    qkv_back, out_back, up_back, down_back, gain_back = fetch_backward(
        qkv_weight, out_weight, up_weight, down_weight, gain_shards
    )
    gain_back = gain_back.astype(jnp.float32)
    gain_back_one, gain_back_two = (gain_back[0], gain_back[1])
    grad_out = cotangent.reshape(rows, width).astype(jnp.float32)
    normed_again, pull_two = jax.vjp(partial(layer_norm, gain=gain_back_two, shift=0.0), hidden_two)
    (grad_two,) = pull_two(grad_out)
    grad_act = jnp.dot(
        grad_two.astype(jnp.bfloat16), down_back.T, preferred_element_type=jnp.float32
    )
    (grad_upper,) = gelu_pull(grad_act)
    grad_normed = grad_two + jnp.dot(
        grad_upper.astype(jnp.bfloat16), up_back.T, preferred_element_type=jnp.float32
    )
    first_again, pull_one = jax.vjp(partial(layer_norm, gain=gain_back_one, shift=0.0), hidden_one)
    (grad_one,) = pull_one(grad_normed)
    grad_mixed = jnp.dot(
        grad_one.astype(jnp.bfloat16), out_back.T, preferred_element_type=jnp.float32
    ).astype(jnp.bfloat16)
    query_rows_gradient, grad_keys, value_rows_gradient = lax.map(
        attend_back,
        (
            queries_heads,
            keys_heads,
            values_heads,
            segment_ids,
            log_total,
            grad_mixed.reshape(head_shape),
        ),
    )
    query_rows_gradient = query_rows_gradient.reshape(rows, width)
    value_rows_gradient = value_rows_gradient.reshape(rows, width)
    grad_project = jnp.concatenate(
        [query_rows_gradient, grad_keys.reshape(rows, width), value_rows_gradient], axis=1
    )
    query_rank_gradient = adapter_scale * jnp.dot(
        query_rows_gradient, query_up_weight.T, preferred_element_type=jnp.float32
    )
    value_rank_gradient = adapter_scale * jnp.dot(
        value_rows_gradient, value_up_weight.T, preferred_element_type=jnp.float32
    )
    grad_rows = grad_one + jnp.dot(grad_project, qkv_back.T, preferred_element_type=jnp.float32)
    grad_rows = grad_rows + jnp.dot(
        query_rank_gradient, query_down.astype(jnp.float32).T, precision=highest_precision_mode
    )
    grad_rows = grad_rows + jnp.dot(
        value_rank_gradient, value_down.astype(jnp.float32).T, precision=highest_precision_mode
    )
    term_query_up = jnp.dot(
        query_rank_rows.T,
        adapter_scale * query_rows_gradient.astype(jnp.float32),
        precision=highest_precision_mode,
    )
    term_value_up = jnp.dot(
        value_rank_rows.T,
        adapter_scale * value_rows_gradient.astype(jnp.float32),
        precision=highest_precision_mode,
    )
    term_query_down = jnp.dot(flat_float.T, query_rank_gradient, precision=highest_precision_mode)
    term_value_down = jnp.dot(flat_float.T, value_rank_gradient, precision=highest_precision_mode)
    sum_query_down, sum_query_up, sum_value_down, sum_value_up = lax.psum(
        (term_query_down, term_query_up, term_value_down, term_value_up), ("dp", "fsdp")
    )
    return (
        output.reshape(packs, seq_len, width),
        grad_rows.reshape(packs, seq_len, width),
        sum_query_down,
        sum_query_up,
        sum_value_down,
        sum_value_up,
    )


def solution(mesh):
    in_specs = (
        P(("dp", "fsdp"), None, None),
        P(("dp", "fsdp"), None),
        P(("dp", "fsdp"), None, None),
        P(("dp", "fsdp"), None),
        P(("dp", "fsdp"), None),
        P(("dp", "fsdp"), None),
        P(("dp", "fsdp"), None),
        P(("dp", "fsdp")),
        P(("dp", "fsdp")),
        P(("dp", "fsdp")),
        P(("dp", "fsdp")),
        P(("dp", "fsdp")),
        P(("dp", "fsdp")),
        P(("dp", "fsdp")),
        P(("dp", "fsdp")),
        P(("dp", "fsdp")),
        P(),
        P(),
        P(),
        P(),
    )
    out_specs = (P(("dp", "fsdp"), None, None), P(("dp", "fsdp"), None, None), P(), P(), P(), P())
    return jax.shard_map(local, mesh=mesh, in_specs=in_specs, out_specs=out_specs, check_vma=False)
```

profile of v0, /device:TPU:8, one launch (start us, length us, event | category | flops | bytes accessed | tf_op | source)
XLA Modules:
  0.0 645.6 jit_solution(10639014909072017310)
XLA Ops:
  11.6 57.1 %all-gather = bf16[32,24,8]{1,2,0:T(8,128)(2,1)S(1)} all-gather(bf16[1,24,8]{1,2,0:T(8,128)(2,1)S(1)} %bitcast.216), channel_id=1, replica_groups=mesh['dp'=8,'fsdp'=4] {'dp','fsdp'}, dimensions={0}, use_global_device_ids=true | all-gather | bytes 12672 | tf_op jit(solution)/shard_map/all_gather | solution.py:30
  73.8 50.2 %all-reduce = bf16[3072]{0:T(1024)(128)(2,1)S(1)} all-reduce(bf16[3072]{0:T(1024)(128)(2,1)S(1)} %dynamic-update-slice), channel_id=1, replica_groups=mesh['dp'=8,'fsdp'=4] {'dp','fsdp'}, use_global_device_ids=true, to_apply=%add | all-reduce | flops 3072 | bytes 12288
  124.7 51.4 %all-gather.1 = bf16[32,24,2]{1,2,0:T(2,128)(2,1)S(1)} all-gather(bf16[1,24,2]{1,2,0:T(2,128)(2,1)S(1)} %maximum_bitcast_fusion), channel_id=1, replica_groups=mesh['dp'=8,'fsdp'=4] {'dp','fsdp'}, dimensions={0}, use_global_device_ids=true | all-gather | bytes 3168 | tf_op jit(solution)/shard_map/all_gather | solution.py:41
  177.0 5.8 fusion.157
  183.0 3.4 copy-done.11
  186.5 2.7 fusion.122
  189.1 2.2 copy.92
  191.3 2.4 reshape.185
  193.7 2.9 copy.95
  196.6 4.6 fusion.120
  202.9 2.4 reshape.186
  208.6 3.8 reshape.187
  214.2 23.0 %while.26 = (s32[]{:T(128)}, bf16[2,512,12,64]{1,3,2,0:T(8,128)(2,1)}, f32[2,12,512]{2,1,0:T(8,128)}, bf16[2,512,12,64]{1,3,2,0:T(8,128)(2,1)}, s32[2,512]{1,0:T...) while((s32[]{:T(128)}, ...), condition=%wide.region_3.4_spmd, body=%wide.region_0.3_spmd.sunk | while | flops 849602560 | bytes 49250932 | solution.py:156
  217.2 3.1 fusion.217
  221.0 4.6 bitcast_dynamic-update-slice_fusion.4
  228.6 3.1 fusion.217
  232.4 4.6 bitcast_dynamic-update-slice_fusion.4
  237.2 3.0 copy.98
  241.8 3.9 fusion.155
  248.0 36.6 %fusion.103 = (f32[1024,3072]{1,0:T(8,128)}, f32[1024,3072]{1,0:T(8,128)}) fusion(f32[3072]{0:T(1024)S(1)} %copy-done.29, bf16[768,3072]{1,0:T(8,128)(2,1)} %all-gather.11.cloned.1.call-done, f32[1024,768]{1,0:T(8,128)} %copy-done.7, f32[768]{0:T(1024)S(1)} %copy-done.31, f32[768]{0:T(1024)S(1)} %copy-done.32, f32[1024]{0:T(1024)S(1)} %fusion.144, ...), kind=kOutput, calls=%fused_computation.80 | convolution fusion | flops 5033951232 | bytes 33056768 | tf_op jit(solution)/shard_map/dot_general | solution.py:166
  284.6 16.2 %fusion.156 = (f32[1024]{0:T(1024)S(1)}, f32[1024,768]{1,0:T(8,128)S(1)}) fusion(f32[768]{0:T(1024)S(1)} %copy-done.30, bf16[3072,768]{1,0:T(8,128)(2,1)} %all-gather.13.cloned.1.call-done, f32[1024,3072]{1,0:T(8,128)} %get-tuple-element.232, f32[1024,3072]{1,0:T(8,128)} %get-tuple-element.233, f32[3072]{0:T(1024)S(1)} %copy-done.29, ...), kind=kOutput, calls=%fused_computation.183 | convolution fusion | flops 4849925120 | bytes 36209664 | tf_op jit(solution)/shard_map/dot_general | solution.py:172
  301.9 3.2 fusion.154
  305.2 23.1 %multiply_reduce_fusion.1 = (f32[1024]{0:T(1024)S(1)}, f32[1024,768]{1,0:T(8,128)}) fusion(f32[1024,768]{1,0:T(8,128)} %copy-done.7, f32[1024]{0:T(1024)S(1)} %broadcast_multiply_fusion.1, f32[768]{0:T(1024)S(1)} %copy-done.34, bf16[768,3072]{1,0:T(8,128)(2,1)} %all-gather.11.cloned.1.call-done, f32[1024,3072]{1,0:T(8,128)} %get-tuple-element.232, ...), kind=kOutput, calls=%fused_computation.126 | convolution fusion | flops 9717152768 | bytes 44067840 | tf_op jit(solution)/shard_map/dot_general | solution.py:189
  328.3 3.6 fusion.153
  333.7 2.6 convolution_convert_fusion
  336.3 2.6 copy.101
  338.9 3.8 reshape.189
  342.7 2.9 copy.104
  345.6 126.3 %while.27 = (s32[]{:T(128)}, bf16[2,512,12,64]{1,3,2,0:T(8,128)(2,1)}, bf16[2,512,12,64]{1,3,2,0:T(8,128)(2,1)}, bf16[2,512,12,64]{1,3,2,0:T(8,128)(2,1)}, bf16[...) while((s32[]{:T(128)}, ...), condition=%wide.region_14.15_spmd, body=%wide.region_12.14_spmd.sunk | while | flops 2096509952 | bytes 160648368 | solution.py:197
  345.8 6.4 fusion.229
  352.2 6.3 fusion.228
  360.2 20.3 %fusion.231 = bf16[2,512,12,64]{1,3,2,0:T(8,128)(2,1)} fusion(bf16[2,512,12,64]{1,3,2,0:T(8,128)(2,1)} %get-tuple-element.383, s32[]{:T(128)} %get-tuple-element.381, f32[12,512,512]{1,2,0:T(8,128)} %fusion.228, f32[12,512,512]{1,2,0:T(8,128)} %fusion.229, f32[12,512]{1,0:T(8,128)S(1)} %dynamic-slice_bitcast_fusion.2, ...), kind=kOutput, calls=%fused_computation.44.clone.1 | convolution fusion | flops 437656064 | bytes 52495360 | tf_op jit(solution)/shard_map/while/body/eval_jaxpr/hqk,qhd->khd/dot_general | solution.py:84
  380.5 20.1 %fusion.230 = bf16[2,512,12,64]{1,3,2,0:T(8,128)(2,1)} fusion(bf16[2,512,12,64]{1,3,2,0:T(8,128)(2,1)} %get-tuple-element.382, s32[]{:T(128)} %get-tuple-element.381, f32[12,512,512]{1,2,0:T(8,128)} %fusion.228, f32[12,512,512]{1,2,0:T(8,128)} %fusion.229, f32[12,512]{1,0:T(8,128)S(1)} %dynamic-slice_bitcast_fusion.2, ...), kind=kOutput, calls=%fused_computation.46.clone.1 | convolution fusion | flops 437656064 | bytes 52495360 | tf_op jit(solution)/shard_map/while/body/eval_jaxpr/hqk,khd->qhd/dot_general | solution.py:81
  400.6 8.3 %fusion.232 = bf16[2,512,12,64]{1,3,2,0:T(8,128)(2,1)} fusion(bf16[2,512,12,64]{1,3,2,0:T(8,128)(2,1)} %get-tuple-element.384, s32[]{:T(128)} %get-tuple-element.381, f32[12,512,512]{1,2,0:T(8,128)} %fusion.229, f32[12,512]{1,0:T(8,128)S(1)} %dynamic-slice_bitcast_fusion.2, pred[512,512]{0,1:T(8,128)(4,1)S(1)} %broadcast_compare_fusion.5, ...), kind=kOutput, calls=%fused_computation.48.clone.1 | convolution fusion | flops 415629312 | bytes 14443520 | tf_op jit(solution)/shard_map/while/body/eval_jaxpr/hqk,qhd->khd/dot_general | solution.py:73
  408.9 6.4 fusion.229
  415.3 6.3 fusion.228
  423.3 20.3 %fusion.231 = bf16[2,512,12,64]{1,3,2,0:T(8,128)(2,1)} fusion(bf16[2,512,12,64]{1,3,2,0:T(8,128)(2,1)} %get-tuple-element.383, s32[]{:T(128)} %get-tuple-element.381, f32[12,512,512]{1,2,0:T(8,128)} %fusion.228, f32[12,512,512]{1,2,0:T(8,128)} %fusion.229, f32[12,512]{1,0:T(8,128)S(1)} %dynamic-slice_bitcast_fusion.2, ...), kind=kOutput, calls=%fused_computation.44.clone.1 | convolution fusion | flops 437656064 | bytes 52495360 | tf_op jit(solution)/shard_map/while/body/eval_jaxpr/hqk,qhd->khd/dot_general | solution.py:84
  443.6 20.1 %fusion.230 = bf16[2,512,12,64]{1,3,2,0:T(8,128)(2,1)} fusion(bf16[2,512,12,64]{1,3,2,0:T(8,128)(2,1)} %get-tuple-element.382, s32[]{:T(128)} %get-tuple-element.381, f32[12,512,512]{1,2,0:T(8,128)} %fusion.228, f32[12,512,512]{1,2,0:T(8,128)} %fusion.229, f32[12,512]{1,0:T(8,128)S(1)} %dynamic-slice_bitcast_fusion.2, ...), kind=kOutput, calls=%fused_computation.46.clone.1 | convolution fusion | flops 437656064 | bytes 52495360 | tf_op jit(solution)/shard_map/while/body/eval_jaxpr/hqk,khd->qhd/dot_general | solution.py:81
  463.7 8.3 %fusion.232 = bf16[2,512,12,64]{1,3,2,0:T(8,128)(2,1)} fusion(bf16[2,512,12,64]{1,3,2,0:T(8,128)(2,1)} %get-tuple-element.384, s32[]{:T(128)} %get-tuple-element.381, f32[12,512,512]{1,2,0:T(8,128)} %fusion.229, f32[12,512]{1,0:T(8,128)S(1)} %dynamic-slice_bitcast_fusion.2, pred[512,512]{0,1:T(8,128)(4,1)S(1)} %broadcast_compare_fusion.5, ...), kind=kOutput, calls=%fused_computation.48.clone.1 | convolution fusion | flops 415629312 | bytes 14443520 | tf_op jit(solution)/shard_map/while/body/eval_jaxpr/hqk,qhd->khd/dot_general | solution.py:73
  472.0 3.0 copy.108
  480.6 2.9 copy.109
  486.7 3.1 fusion.160
  489.8 2.4 fusion.126
  492.2 2.4 fusion.129
  495.9 3.1 copy.107
  500.7 6.6 %fusion.113 = f32[1024,768]{1,0:T(8,128)S(1)} fusion(bf16[768,2304]{1,0:T(8,128)(2,1)} %all-gather.7.cloned.1.call-done, bf16[1024,768]{0,1:T(8,128)(2,1)S(1)} %bitcast.200, bf16[1024,768]{0,1:T(8,128)(2,1)} %bitcast.210, bf16[1024,768]{0,1:T(8,128)(2,1)S(1)} %bitcast.203), kind=kOutput, calls=%fused_computation.102 | convolution fusion | flops 3638034432 | bytes 11403264 | tf_op jit(solution)/shard_map/dot_general | solution.py:219
  507.3 3.5 add_add_fusion.2
  510.8 122.5 %all-reduce.4.cloned.1.call-done = (f32[768,8]{0,1:T(8,128)}, f32[8,768]{1,0:T(8,128)}, f32[768,8]{0,1:T(8,128)}, f32[8,768]{1,0:T(8,128)}) async-done(((f32[768,8]{0,1:T(8,128)}, f32[8,768]{1,0:T(8,128)}, f32[768,8]{0,1:T(8,128)}, f32[8,768]{1,0:T(8,128)}), (f32[768,8]{0,1:T(8,128)}, f32[8,768]{1,0:T(8,128)}, f32[768,8]{0,1:T(8,128)}, f32[8,768]{1,0:T(8,128)})) %all-reduce.4.cloned.1.call-update) | async-done | bytes 98320 | tf_op jit(solution)/shard_map/psum | solution.py:238
  (155 shorter events, 52.1 us)
Async XLA Ops:
  7.2 179.3 %copy-start = (bf16[8,768]{1,0:T(8,128)(2,1)S(1)}, bf16[8,768]{1,0:T(8,128)(2,1)}, u32[]{:S(2)}) copy-start(bf16[8,768]{1,0:T(8,128)(2,1)} %param.43) | copy-start | bytes 36868
  7.2 169.8 %copy-start.1 = (bf16[2,512,768]{2,1,0:T(8,128)(2,1)S(1)}, bf16[2,512,768]{2,1,0:T(8,128)(2,1)}, u32[]{:S(2)}) copy-start(bf16[2,512,768]{2,1,0:T(8,128)(2,1)} %param.24) | copy-start | bytes 4718596
  7.2 66.4 %copy-start.36 = (bf16[96]{0:T(256)(128)(2,1)S(1)}, bf16[96]{0:T(256)(128)(2,1)}, u32[]{:S(2)}) copy-start(bf16[96]{0:T(256)(128)(2,1)} %param.36) | copy-start | bytes 580
  7.2 169.8 %all-gather.7.cloned.1.call-start = ((), (), s32[]{:S(2)}) async-start(), calls=%async_computation | async-start | bytes 3649536 | tf_op jit(solution)/shard_map/all_gather | solution.py:26
  7.9 233.8 %all-gather.9.cloned.1.call-start = ((), (), s32[]{:S(2)}) async-start(), calls=%async_computation.1 | async-start | bytes 1216512 | tf_op jit(solution)/shard_map/all_gather | solution.py:27
  8.7 239.2 %all-gather.11.cloned.1.call-start = ((), (), s32[]{:S(2)}) async-start(), calls=%async_computation.2 | async-start | bytes 4866048 | tf_op jit(solution)/shard_map/all_gather | solution.py:28
  9.4 275.1 %all-gather.13.cloned.1.call-start = ((), (), s32[]{:S(2)}) async-start(), calls=%async_computation.3 | async-start | bytes 4866048 | tf_op jit(solution)/shard_map/all_gather | solution.py:29
  10.0 623.3 %all-reduce.4.cloned.1.call-start = ((), (), s32[]{:S(2)}) async-start(), calls=%async_computation.4 | async-start | bytes 196608 | tf_op jit(solution)/shard_map/psum | solution.py:238
  71.6 111.4 %copy-start.18 = (f32[1024,8]{0,1:T(8,128)}, f32[1024,8]{0,1:T(8,128)S(1)}, u32[]{:S(2)}) copy-start(f32[1024,8]{0,1:T(8,128)S(1)} %fusion.158) | copy-start | bytes 98308
  73.5 123.0 %copy-start.16 = (f32[1024,8]{0,1:T(8,128)}, f32[1024,8]{0,1:T(8,128)S(1)}, u32[]{:S(2)}) copy-start(f32[1024,8]{0,1:T(8,128)S(1)} %fusion.159) | copy-start | bytes 98308
  182.8 3.6 copy-start.11
  191.3 5.3 copy-start.20
  217.2 3.8 copy-start.3
  228.6 3.8 copy-start.3
  237.1 4.6 copy-start.33
  245.7 1.7 copy-start.7
  245.7 2.2 copy-start.29
  245.7 2.2 copy-start.31
  245.7 2.2 copy-start.32
  247.9 36.6 %copy-start.30 = (f32[768]{0:T(1024)S(1)}, f32[768]{0:T(1024)}, u32[]{:S(2)}) copy-start(f32[768]{0:T(1024)} %get-tuple-element.175) | copy-start | bytes 9220
  284.6 16.3 %copy-start.12 = (bf16[2,512,768]{2,1,0:T(8,128)(2,1)S(1)}, bf16[2,512,768]{2,1,0:T(8,128)(2,1)}, u32[]{:S(2)}) copy-start(bf16[2,512,768]{2,1,0:T(8,128)(2,1)} %param.26) | copy-start | bytes 4718596
  284.6 16.3 %copy-start.24 = (f32[768]{0:T(1024)S(1)}, f32[768]{0:T(1024)}, u32[]{:S(2)}) copy-start(f32[768]{0:T(1024)} %get-tuple-element.182) | copy-start | bytes 9220
  300.8 1.1 copy-start.25
  300.8 1.1 copy-start.26
  301.9 3.3 copy-start.34
  328.3 5.3 copy-start.35
  331.9 1.8 copy-start.9
  331.9 1.7 copy-start.27
  345.8 6.4 copy-start.4
  345.8 6.4 copy-start.5
  408.9 6.4 copy-start.4
  408.9 6.4 copy-start.5
  475.4 1.9 copy-start.15
  478.9 4.5 copy-start.21
  480.6 4.8 copy-start.2
  480.6 6.1 copy-start.22
  483.5 6.3 copy-start.13
  483.5 6.3 copy-start.19
  485.4 6.8 %copy-start.14 = (bf16[1024,768]{1,0:T(8,128)(2,1)S(1)}, bf16[1024,768]{1,0:T(8,128)(2,1)}, u32[]{:S(2)}) copy-start(bf16[1024,768]{1,0:T(8,128)(2,1)} %copy.109) | copy-start | bytes 4718596
  485.4 6.8 %copy-start.17 = (f32[1024,8]{0,1:T(8,128)S(1)}, f32[1024,8]{0,1:T(8,128)}, u32[]{:S(2)}) copy-start(f32[1024,8]{0,1:T(8,128)} %copy-done.16) | copy-start | bytes 98308
  495.9 4.8 copy-start.6
  500.7 6.6 %copy-start.8 = (f32[1024,768]{1,0:T(8,128)S(1)}, f32[1024,768]{1,0:T(8,128)}, u32[]{:S(2)}) copy-start(f32[1024,768]{1,0:T(8,128)} %fusion.160) | copy-start | bytes 9437188
  500.7 6.6 %copy-start.10 = (f32[1024,768]{1,0:T(8,128)S(1)}, f32[1024,768]{1,0:T(8,128)}, u32[]{:S(2)}) copy-start(f32[1024,768]{1,0:T(8,128)} %copy-done.9) | copy-start | bytes 9437188
  500.7 6.6 %copy-start.23 = (bf16[768,8]{0,1:T(8,128)(2,1)S(1)}, bf16[768,8]{0,1:T(8,128)(2,1)}, u32[]{:S(2)}) copy-start(bf16[768,8]{0,1:T(8,128)(2,1)} %param.42) | copy-start | bytes 36868
  500.7 6.6 %copy-start.28 = (f32[1024]{0:T(1024)S(1)}, f32[1024]{0:T(1024)}, u32[]{:S(2)}) copy-start(f32[1024]{0:T(1024)} %copy-done.27) | copy-start | bytes 12292
Sparse Core Ops, SparseCore 0:
  10.9 61.1 all-gather.6
  75.0 52.4 all-gather.8
  130.4 64.2 all-gather.10
  197.4 62.3 all-gather.12
  500.8 132.4 all-reduce.3
where the time goes:
time: 652 us; the launch traced here: 646 us
  matrix products  258 us (40%)
  blocking collectives  159 us (24%)
  waiting for transfers between devices  125 us (19%)
  local copies, waits for them, and re-layouts  70 us (11%)
  other arithmetic  18.1 us (3%)
  between operations  14.7 us (2%)
    psum x1, waiting for transfers between devices, local(): lax.psum((term_query_down, term_query_up, term_value_down, term_value_up)...  123 us
    all_gather x1, blocking collectives, fetch_forward(): lax.all_gather(vectors, ('dp', 'fsdp'), axis=1, tiled=True)  57.1 us
    all_gather x1, blocking collectives, fetch_backward(): lax.all_gather(gains, ('dp', 'fsdp'), axis=1, tiled=True)  51.4 us
    unnamed x1, blocking collectives  50.2 us
    dot_general x2, matrix products, attend_back(): jnp.einsum('hqk,qhd->khd', grad_raw, query_rows, preferred_element_type=j...  40.7 us
    dot_general x2, matrix products, attend_back(): jnp.einsum('hqk,khd->qhd', grad_raw, key_rows, preferred_element_type=jnp...  40.1 us
    dot_general x1, matrix products, local(): jnp.dot(normed_one.astype(jnp.bfloat16), up_full, preferred_element_type=...  36.6 us
    dot_general x1, matrix products, local(): jnp.dot(grad_upper.astype(jnp.bfloat16), up_back.T, preferred_element_typ...  23.1 us
  transfers between devices with their start and end apart: 5, of which 1 were waited for; matrix products, arithmetic and copies ran while one was open for 19% of the time, Pallas kernels for 0%

commit v1 on v0

--- a/solution.py
+++ b/solution.py
@@ -9,6 +9,18 @@
 highest_precision_mode = lax.Precision.HIGHEST
 norm_epsilon = 1e-05
 adapter_scale = 2.0
+
+
+def gather_by_bits(x, axis, dim):
+    ways, here, turn = (lax.axis_size(axis), lax.axis_index(axis), x.shape[dim])
+    line, have = (x, 1)
+    while have < ways:
+        line = jnp.concatenate(
+            [line, lax.ppermute(line, axis, [(d, (d - have) % ways) for d in range(ways)])],
+            axis=dim,
+        )
+        have = 2 * have
+    return jnp.roll(line, here * turn, axis=dim)
 
 
 def layer_norm(value_rows, gain, shift):
@@ -38,7 +50,7 @@
         lax.all_gather(out_weight, ("dp", "fsdp"), axis=0, tiled=True),
         lax.all_gather(up_weight, ("dp", "fsdp"), axis=0, tiled=True),
         lax.all_gather(down_weight, ("dp", "fsdp"), axis=0, tiled=True),
-        lax.all_gather(gains, ("dp", "fsdp"), axis=1, tiled=True),
+        gather_by_bits(gains, ("dp", "fsdp"), 1),
     )
 
 

time: 652 us -> 620 us (0.951)
  blocking collectives: 159 us -> 96.9 us
  starting transfers between devices: 0.19 us -> 19 us
  waiting for transfers between devices: 125 us -> 133 us
    all_gather x1 -> x0, blocking collectives: 51.4 us -> none  [fetch_backward(): lax.all_gather(gains, ('dp', 'fsdp'), axis=1, tiled=True)]
    ppermute x0 -> x5, starting transfers between devices: none -> 18.8 us  [gather_by_bits(): lax.ppermute(line, axis, [(d, (d - have) % ways) for d in range(ways)])]
    all_gather x1, waiting for transfers between devices: 0.01 us -> 14.5 us  [fetch_forward(): lax.all_gather(down_weight, ('dp', 'fsdp'), axis=0, tiled=True)]
    psum x1, waiting for transfers between devices: 123 us -> 112 us  [local(): lax.psum((term_query_down, term_query_up, term_value_down, term_value_up)...]
    unnamed x1, blocking collectives: 50.2 us -> 41.1 us
    unnamed x78 -> x82, local copies, waits for them, and re-layouts: 17.8 us -> 17.8 us
  transfers between devices with their start and end apart: 5 -> 10, of which waited for: 1 -> 5; matrix products, arithmetic and copies ran while one was open for 19% -> 20% of each run, Pallas kernels for 0% -> 0%
where the time goes in v1:
time: 620 us; the launch traced here: 610 us
  matrix products  258 us (42%)
  waiting for transfers between devices  133 us (21%)
  blocking collectives  96.9 us (16%)
  local copies, waits for them, and re-layouts  69.2 us (11%)
  starting transfers between devices  19 us (3%)
  other arithmetic  18.8 us (3%)
  between operations  14.7 us (2%)
    psum x1, waiting for transfers between devices, local(): lax.psum((term_query_down, term_query_up, term_value_down, term_value_up)...  112 us
    all_gather x1, blocking collectives, fetch_forward(): lax.all_gather(vectors, ('dp', 'fsdp'), axis=1, tiled=True)  55.8 us
    unnamed x1, blocking collectives  41.1 us
    dot_general x2, matrix products, attend_back(): jnp.einsum('hqk,qhd->khd', grad_raw, query_rows, preferred_element_type=j...  40.5 us
    dot_general x2, matrix products, attend_back(): jnp.einsum('hqk,khd->qhd', grad_raw, key_rows, preferred_element_type=jnp...  40.1 us
    dot_general x1, matrix products, local(): jnp.dot(normed_one.astype(jnp.bfloat16), up_full, preferred_element_type=...  36.8 us
    dot_general x1, matrix products, local(): jnp.dot(grad_upper.astype(jnp.bfloat16), up_back.T, preferred_element_typ...  23.1 us
    ppermute x5, starting transfers between devices, gather_by_bits(): lax.ppermute(line, axis, [(d, (d - have) % ways) for d in range(ways)])  18.8 us
  transfers between devices with their start and end apart: 10, of which 5 were waited for; matrix products, arithmetic and copies ran while one was open for 20% of the time, Pallas kernels for 0%

profile of v1, /device:TPU:8, one launch (start us, length us, event | category | flops | bytes accessed | tf_op | source)
XLA Modules:
  0.0 610.1 jit_solution(5498351245723242659)
XLA Ops:
  12.9 55.8 %all-gather = bf16[32,24,8]{1,2,0:T(8,128)(2,1)S(1)} all-gather(bf16[1,24,8]{1,2,0:T(8,128)(2,1)S(1)} %bitcast.208), channel_id=1, replica_groups=mesh['dp'=8,'fsdp'=4] {'dp','fsdp'}, dimensions={0}, use_global_device_ids=true | all-gather | bytes 12672 | tf_op jit(solution)/shard_map/all_gather | solution.py:42
  73.7 3.8 collective-permute-start.1
  78.8 6.2 %collective-permute-start.2 = (bf16[2,96]{1,0:T(2,128)(2,1)S(1)}, bf16[2,96]{1,0:T(2,128)(2,1)S(1)}, u32[]{:S(2)}, u32[]{:S(2)}) collective-permute-start(bf16[2,96]{1,0:T(2,128)(2,1)S(1)} %pad_maximum_fusion.3), channel_id=1, source_target_pairs={{0,28},{1,29},{2,30},{3,31},{4,0},{5,1},{6,2},{7,3},{8,4},{9,5},{1... | collective-permute-start | bytes 1160 | tf_op jit(solution)/shard_map/ppermute | solution.py:19
  86.4 4.4 collective-permute-start.3
  92.2 2.7 collective-permute-start.4
  94.8 41.1 %all-reduce = bf16[3072]{0:T(1024)(128)(2,1)S(1)} all-reduce(bf16[3072]{0:T(1024)(128)(2,1)S(1)} %dynamic-update-slice), channel_id=1, replica_groups=mesh['dp'=8,'fsdp'=4] {'dp','fsdp'}, use_global_device_ids=true, to_apply=%add | all-reduce | flops 3072 | bytes 12288
  137.4 5.9 fusion.157
  143.5 3.4 copy-done.11
  146.9 2.7 fusion.122
  151.3 2.4 reshape.185
  153.7 2.9 copy.93
  156.6 4.6 fusion.120
  168.6 3.8 reshape.187
  174.2 23.0 %while.26 = (s32[]{:T(128)}, bf16[2,512,12,64]{1,3,2,0:T(8,128)(2,1)}, f32[2,12,512]{2,1,0:T(8,128)}, bf16[2,512,12,64]{1,3,2,0:T(8,128)(2,1)}, s32[2,512]{1,0:T...) while((s32[]{:T(128)}, ...), condition=%wide.region_3.4_spmd, body=%wide.region_0.3_spmd.sunk | while | flops 849602560 | bytes 49250932 | solution.py:168
  177.4 3.1 fusion.217
  181.2 4.6 bitcast_dynamic-update-slice_fusion.4
  188.8 3.1 fusion.217
  192.6 4.6 bitcast_dynamic-update-slice_fusion.4
  197.2 3.0 copy.96
  201.8 4.0 fusion.155
  208.1 36.8 %fusion.103 = (f32[1024,3072]{1,0:T(8,128)}, f32[1024,3072]{1,0:T(8,128)}) fusion(f32[3072]{0:T(1024)S(1)} %copy-done.29, bf16[768,3072]{1,0:T(8,128)(2,1)} %all-gather.10.cloned.1.call-done, f32[1024,768]{1,0:T(8,128)} %copy-done.7, f32[768]{0:T(1024)S(1)} %copy-done.33, f32[768]{0:T(1024)S(1)} %copy-done.34, f32[1024]{0:T(1024)S(1)} %fusion.144, ...), kind=kOutput, calls=%fused_computation.80 | convolution fusion | flops 5033951232 | bytes 33056768 | tf_op jit(solution)/shard_map/dot_general | solution.py:178
  244.9 14.5 %all-gather.12.cloned.1.call-done = bf16[3072,768]{1,0:T(8,128)(2,1)} async-done(((bf16[96,768]{1,0:T(8,128)(2,1)}), bf16[3072,768]{1,0:T(8,128)(2,1)}) %all-gather.12.cloned.1.call-update) | async-done | bytes 4718608 | tf_op jit(solution)/shard_map/all_gather | solution.py:41
  259.4 15.9 %fusion.156 = (f32[1024]{0:T(1024)S(1)}, f32[1024,768]{1,0:T(8,128)S(1)}) fusion(f32[768]{0:T(1024)S(1)} %copy-done.32, bf16[3072,768]{1,0:T(8,128)(2,1)} %all-gather.12.cloned.1.call-done, f32[1024,3072]{1,0:T(8,128)} %get-tuple-element.232, f32[1024,3072]{1,0:T(8,128)} %get-tuple-element.233, f32[3072]{0:T(1024)S(1)} %copy-done.29, ...), kind=kOutput, calls=%fused_computation.187 | convolution fusion | flops 4849925120 | bytes 36209664 | tf_op jit(solution)/shard_map/dot_general | solution.py:184
  276.4 3.6 fusion.154
  280.0 23.1 %multiply_reduce_fusion.1 = (f32[1024]{0:T(1024)S(1)}, f32[1024,768]{1,0:T(8,128)}) fusion(f32[1024,768]{1,0:T(8,128)} %copy-done.7, f32[1024]{0:T(1024)S(1)} %broadcast_multiply_fusion.1, f32[768]{0:T(1024)S(1)} %copy-done.36, bf16[768,3072]{1,0:T(8,128)(2,1)} %all-gather.10.cloned.1.call-done, f32[1024,3072]{1,0:T(8,128)} %get-tuple-element.232, ...), kind=kOutput, calls=%fused_computation.126 | convolution fusion | flops 9717152768 | bytes 44067840 | tf_op jit(solution)/shard_map/dot_general | solution.py:201
  303.1 3.6 fusion.153
  308.5 2.6 convolution_convert_fusion
  311.1 2.6 copy.97
  313.7 3.8 reshape.189
  317.5 2.9 copy.100
  320.4 126.4 %while.27 = (s32[]{:T(128)}, bf16[2,512,12,64]{1,3,2,0:T(8,128)(2,1)}, bf16[2,512,12,64]{1,3,2,0:T(8,128)(2,1)}, bf16[2,512,12,64]{1,3,2,0:T(8,128)(2,1)}, bf16[...) while((s32[]{:T(128)}, ...), condition=%wide.region_14.15_spmd, body=%wide.region_12.14_spmd.sunk | while | flops 2096509952 | bytes 160648368 | solution.py:209
  320.6 6.4 %fusion.229 = f32[12,512,512]{1,2,0:T(8,128)} fusion(bf16[2,512,12,64]{1,3,2,0:T(8,128)(2,1)S(1)} %get-tuple-element.398, s32[]{:T(128)} %get-tuple-element.381, bf16[2,512,12,64]{1,3,2,0:T(8,128)(2,1)S(1)} %get-tuple-element.396), kind=kOutput, calls=%fused_computation.54.clone.1 | convolution fusion | flops 402653184 | bytes 14156800 | tf_op jit(solution)/shard_map/while/body/eval_jaxpr/qhd,khd->hqk/dot_general | solution.py:80
  327.0 6.3 %fusion.228 = f32[12,512,512]{1,2,0:T(8,128)} fusion(bf16[2,512,12,64]{1,3,2,0:T(8,128)(2,1)S(1)} %copy-done.4, s32[]{:T(128)} %get-tuple-element.381, bf16[2,512,12,64]{1,3,2,0:T(8,128)(2,1)S(1)} %copy-done.5), kind=kOutput, calls=%fused_computation.49.clone.1 | convolution fusion | flops 402653184 | bytes 14156800 | tf_op jit(solution)/shard_map/while/body/eval_jaxpr/qhd,khd->hqk/dot_general | solution.py:88
  335.0 20.3 %fusion.231 = bf16[2,512,12,64]{1,3,2,0:T(8,128)(2,1)} fusion(bf16[2,512,12,64]{1,3,2,0:T(8,128)(2,1)} %get-tuple-element.383, s32[]{:T(128)} %get-tuple-element.381, f32[12,512,512]{1,2,0:T(8,128)} %fusion.228, f32[12,512,512]{1,2,0:T(8,128)} %fusion.229, f32[12,512]{1,0:T(8,128)S(1)} %dynamic-slice_bitcast_fusion.2, ...), kind=kOutput, calls=%fused_computation.44.clone.1 | convolution fusion | flops 437656064 | bytes 52495360 | tf_op jit(solution)/shard_map/while/body/eval_jaxpr/hqk,qhd->khd/dot_general | solution.py:96
  355.3 20.1 %fusion.230 = bf16[2,512,12,64]{1,3,2,0:T(8,128)(2,1)} fusion(bf16[2,512,12,64]{1,3,2,0:T(8,128)(2,1)} %get-tuple-element.382, s32[]{:T(128)} %get-tuple-element.381, f32[12,512,512]{1,2,0:T(8,128)} %fusion.228, f32[12,512,512]{1,2,0:T(8,128)} %fusion.229, f32[12,512]{1,0:T(8,128)S(1)} %dynamic-slice_bitcast_fusion.2, ...), kind=kOutput, calls=%fused_computation.46.clone.1 | convolution fusion | flops 437656064 | bytes 52495360 | tf_op jit(solution)/shard_map/while/body/eval_jaxpr/hqk,khd->qhd/dot_general | solution.py:93
  375.3 8.3 %fusion.232 = bf16[2,512,12,64]{1,3,2,0:T(8,128)(2,1)} fusion(bf16[2,512,12,64]{1,3,2,0:T(8,128)(2,1)} %get-tuple-element.384, s32[]{:T(128)} %get-tuple-element.381, f32[12,512,512]{1,2,0:T(8,128)} %fusion.229, f32[12,512]{1,0:T(8,128)S(1)} %dynamic-slice_bitcast_fusion.2, pred[512,512]{0,1:T(8,128)(4,1)S(1)} %broadcast_compare_fusion.5, ...), kind=kOutput, calls=%fused_computation.48.clone.1 | convolution fusion | flops 415629312 | bytes 14443520 | tf_op jit(solution)/shard_map/while/body/eval_jaxpr/hqk,qhd->khd/dot_general | solution.py:85
  383.6 6.4 %fusion.229 = f32[12,512,512]{1,2,0:T(8,128)} fusion(bf16[2,512,12,64]{1,3,2,0:T(8,128)(2,1)S(1)} %get-tuple-element.398, s32[]{:T(128)} %get-tuple-element.381, bf16[2,512,12,64]{1,3,2,0:T(8,128)(2,1)S(1)} %get-tuple-element.396), kind=kOutput, calls=%fused_computation.54.clone.1 | convolution fusion | flops 402653184 | bytes 14156800 | tf_op jit(solution)/shard_map/while/body/eval_jaxpr/qhd,khd->hqk/dot_general | solution.py:80
  390.0 6.3 %fusion.228 = f32[12,512,512]{1,2,0:T(8,128)} fusion(bf16[2,512,12,64]{1,3,2,0:T(8,128)(2,1)S(1)} %copy-done.4, s32[]{:T(128)} %get-tuple-element.381, bf16[2,512,12,64]{1,3,2,0:T(8,128)(2,1)S(1)} %copy-done.5), kind=kOutput, calls=%fused_computation.49.clone.1 | convolution fusion | flops 402653184 | bytes 14156800 | tf_op jit(solution)/shard_map/while/body/eval_jaxpr/qhd,khd->hqk/dot_general | solution.py:88
  398.0 20.3 %fusion.231 = bf16[2,512,12,64]{1,3,2,0:T(8,128)(2,1)} fusion(bf16[2,512,12,64]{1,3,2,0:T(8,128)(2,1)} %get-tuple-element.383, s32[]{:T(128)} %get-tuple-element.381, f32[12,512,512]{1,2,0:T(8,128)} %fusion.228, f32[12,512,512]{1,2,0:T(8,128)} %fusion.229, f32[12,512]{1,0:T(8,128)S(1)} %dynamic-slice_bitcast_fusion.2, ...), kind=kOutput, calls=%fused_computation.44.clone.1 | convolution fusion | flops 437656064 | bytes 52495360 | tf_op jit(solution)/shard_map/while/body/eval_jaxpr/hqk,qhd->khd/dot_general | solution.py:96
  418.3 20.0 %fusion.230 = bf16[2,512,12,64]{1,3,2,0:T(8,128)(2,1)} fusion(bf16[2,512,12,64]{1,3,2,0:T(8,128)(2,1)} %get-tuple-element.382, s32[]{:T(128)} %get-tuple-element.381, f32[12,512,512]{1,2,0:T(8,128)} %fusion.228, f32[12,512,512]{1,2,0:T(8,128)} %fusion.229, f32[12,512]{1,0:T(8,128)S(1)} %dynamic-slice_bitcast_fusion.2, ...), kind=kOutput, calls=%fused_computation.46.clone.1 | convolution fusion | flops 437656064 | bytes 52495360 | tf_op jit(solution)/shard_map/while/body/eval_jaxpr/hqk,khd->qhd/dot_general | solution.py:93
  438.3 8.3 %fusion.232 = bf16[2,512,12,64]{1,3,2,0:T(8,128)(2,1)} fusion(bf16[2,512,12,64]{1,3,2,0:T(8,128)(2,1)} %get-tuple-element.384, s32[]{:T(128)} %get-tuple-element.381, f32[12,512,512]{1,2,0:T(8,128)} %fusion.229, f32[12,512]{1,0:T(8,128)S(1)} %dynamic-slice_bitcast_fusion.2, pred[512,512]{0,1:T(8,128)(4,1)S(1)} %broadcast_compare_fusion.5, ...), kind=kOutput, calls=%fused_computation.48.clone.1 | convolution fusion | flops 415629312 | bytes 14443520 | tf_op jit(solution)/shard_map/while/body/eval_jaxpr/hqk,qhd->khd/dot_general | solution.py:85
  446.8 3.0 copy.104
  455.4 2.7 copy.105
  461.3 3.1 fusion.160
  470.5 3.1 copy.103
  475.3 6.6 %fusion.113 = f32[1024,768]{1,0:T(8,128)S(1)} fusion(bf16[768,2304]{1,0:T(8,128)(2,1)} %all-gather.6.cloned.1.call-done, bf16[1024,768]{0,1:T(8,128)(2,1)S(1)} %bitcast.193, bf16[1024,768]{0,1:T(8,128)(2,1)} %bitcast.203, bf16[1024,768]{0,1:T(8,128)(2,1)S(1)} %bitcast.196), kind=kOutput, calls=%fused_computation.102 | convolution fusion | flops 3638034432 | bytes 11403264 | tf_op jit(solution)/shard_map/dot_general | solution.py:231
  481.9 3.5 add_add_fusion.2
  485.4 112.4 %all-reduce.4.cloned.1.call-done = (f32[768,8]{0,1:T(8,128)}, f32[8,768]{1,0:T(8,128)}, f32[768,8]{0,1:T(8,128)}, f32[8,768]{1,0:T(8,128)}) async-done(((f32[768,8]{0,1:T(8,128)}, f32[8,768]{1,0:T(8,128)}, f32[768,8]{0,1:T(8,128)}, f32[8,768]{1,0:T(8,128)}), (f32[768,8]{0,1:T(8,128)}, f32[8,768]{1,0:T(8,128)}, f32[768,8]{0,1:T(8,128)}, f32[8,768]{1,0:T(8,128)})) %all-reduce.4.cloned.1.call-update) | async-done | bytes 98320 | tf_op jit(solution)/shard_map/psum | solution.py:250
  (171 shorter events, 66.1 us)
Async XLA Ops:
  7.2 139.8 %copy-start = (bf16[8,768]{1,0:T(8,128)(2,1)S(1)}, bf16[8,768]{1,0:T(8,128)(2,1)}, u32[]{:S(2)}) copy-start(bf16[8,768]{1,0:T(8,128)(2,1)} %param.43) | copy-start | bytes 36868
  7.2 66.4 %copy-start.30 = (bf16[24]{0:T(256)(128)(2,1)S(1)}, bf16[24]{0:T(256)(128)(2,1)}, u32[]{:S(2)}) copy-start(bf16[24]{0:T(256)(128)(2,1)} %param.34) | copy-start | bytes 148
  7.2 66.4 %copy-start.31 = (bf16[24]{0:T(256)(128)(2,1)S(1)}, bf16[24]{0:T(256)(128)(2,1)}, u32[]{:S(2)}) copy-start(bf16[24]{0:T(256)(128)(2,1)} %param.38) | copy-start | bytes 148
  7.2 130.2 %copy-start.1 = (bf16[2,512,768]{2,1,0:T(8,128)(2,1)S(1)}, bf16[2,512,768]{2,1,0:T(8,128)(2,1)}, u32[]{:S(2)}) copy-start(bf16[2,512,768]{2,1,0:T(8,128)(2,1)} %param.24) | copy-start | bytes 4718596
  7.2 83.6 %copy-start.38 = (bf16[96]{0:T(256)(128)(2,1)S(1)}, bf16[96]{0:T(256)(128)(2,1)}, u32[]{:S(2)}) copy-start(bf16[96]{0:T(256)(128)(2,1)} %param.36) | copy-start | bytes 580
  7.2 130.1 %all-gather.6.cloned.1.call-start = ((), (), s32[]{:S(2)}) async-start(), calls=%async_computation | async-start | bytes 3649536 | tf_op jit(solution)/shard_map/all_gather | solution.py:38
  8.0 193.8 %all-gather.8.cloned.1.call-start = ((), (), s32[]{:S(2)}) async-start(), calls=%async_computation.1 | async-start | bytes 1216512 | tf_op jit(solution)/shard_map/all_gather | solution.py:39
  8.7 199.3 %all-gather.10.cloned.1.call-start = ((), (), s32[]{:S(2)}) async-start(), calls=%async_computation.2 | async-start | bytes 4866048 | tf_op jit(solution)/shard_map/all_gather | solution.py:40
  9.4 249.9 %all-gather.12.cloned.1.call-start = ((), (), s32[]{:S(2)}) async-start(), calls=%async_computation.3 | async-start | bytes 4866048 | tf_op jit(solution)/shard_map/all_gather | solution.py:41
  10.2 63.4 %collective-permute-start = (bf16[2,24]{1,0:T(2,128)(2,1)S(1)}, bf16[2,24]{1,0:T(2,128)(2,1)S(1)}, u32[]{:S(2)}, u32[]{:S(2)}) collective-permute-start(bf16[2,24]{1,0:T(2,128)(2,1)S(1)} %pad_maximum_fusion.1), channel_id=1, source_target_pairs={{0,31},{1,0},{2,1},{3,2},{4,3},{5,4},{6,5},{7,6},{8,7},{9,8},{10,9... | collective-permute-start | bytes 296 | tf_op jit(solution)/shard_map/ppermute | solution.py:19
  12.0 585.8 %all-reduce.4.cloned.1.call-start = ((), (), s32[]{:S(2)}) async-start(), calls=%async_computation.4 | async-start | bytes 196608 | tf_op jit(solution)/shard_map/psum | solution.py:250
  71.6 71.9 %copy-start.18 = (f32[1024,8]{0,1:T(8,128)}, f32[1024,8]{0,1:T(8,128)S(1)}, u32[]{:S(2)}) copy-start(f32[1024,8]{0,1:T(8,128)S(1)} %fusion.158) | copy-start | bytes 98308
  73.5 83.0 %copy-start.16 = (f32[1024,8]{0,1:T(8,128)}, f32[1024,8]{0,1:T(8,128)S(1)}, u32[]{:S(2)}) copy-start(f32[1024,8]{0,1:T(8,128)S(1)} %fusion.159) | copy-start | bytes 98308
  73.7 5.1 collective-permute-start.1
  78.8 7.5 %collective-permute-start.2 = (bf16[2,96]{1,0:T(2,128)(2,1)S(1)}, bf16[2,96]{1,0:T(2,128)(2,1)S(1)}, u32[]{:S(2)}, u32[]{:S(2)}) collective-permute-start(bf16[2,96]{1,0:T(2,128)(2,1)S(1)} %pad_maximum_fusion.3), channel_id=1, source_target_pairs={{0,28},{1,29},{2,30},{3,31},{4,0},{5,1},{6,2},{7,3},{8,4},{9,5},{1... | collective-permute-start | bytes 1160 | tf_op jit(solution)/shard_map/ppermute | solution.py:19
  86.4 5.7 collective-permute-start.3
  92.2 44.4 %collective-permute-start.4 = (bf16[2,384]{1,0:T(2,128)(2,1)S(1)}, bf16[2,384]{1,0:T(2,128)(2,1)S(1)}, u32[]{:S(2)}, u32[]{:S(2)}) collective-permute-start(bf16[2,384]{1,0:T(2,128)(2,1)S(1)} %concatenate.28), channel_id=1, source_target_pairs={{0,16},{1,17},{2,18},{3,19},{4,20},{5,21},{6,22},{7,23},{8,24},{9,... | collective-permute-start | bytes 4616 | tf_op jit(solution)/shard_map/ppermute | solution.py:19
  143.3 3.6 copy-start.11
  151.3 5.3 copy-start.20
  177.4 3.8 copy-start.3
  188.8 3.8 copy-start.3
  197.2 4.6 copy-start.35
  205.8 2.2 copy-start.29
  205.8 2.2 copy-start.33
  205.8 2.2 copy-start.34
  208.0 51.3 %copy-start.32 = (f32[768]{0:T(1024)S(1)}, f32[768]{0:T(1024)}, u32[]{:S(2)}) copy-start(f32[768]{0:T(1024)} %get-tuple-element.175) | copy-start | bytes 9220
  259.4 15.9 %copy-start.12 = (bf16[2,512,768]{2,1,0:T(8,128)(2,1)S(1)}, bf16[2,512,768]{2,1,0:T(8,128)(2,1)}, u32[]{:S(2)}) copy-start(bf16[2,512,768]{2,1,0:T(8,128)(2,1)} %param.26) | copy-start | bytes 4718596
  259.4 15.9 %copy-start.24 = (f32[768]{0:T(1024)S(1)}, f32[768]{0:T(1024)}, u32[]{:S(2)}) copy-start(f32[768]{0:T(1024)} %get-tuple-element.182) | copy-start | bytes 9220
  276.4 3.7 copy-start.36
  303.1 5.3 copy-start.37
  306.7 1.8 copy-start.9
  320.6 6.4 %copy-start.4 = (bf16[2,512,12,64]{1,3,2,0:T(8,128)(2,1)S(1)}, bf16[2,512,12,64]{1,3,2,0:T(8,128)(2,1)}, u32[]{:S(2)}) copy-start(bf16[2,512,12,64]{1,3,2,0:T(8,128)(2,1)} %get-tuple-element.401) | copy-start | bytes 4718596 | tf_op jit(solution)/shard_map/while
  320.6 6.4 %copy-start.5 = (bf16[2,512,12,64]{1,3,2,0:T(8,128)(2,1)S(1)}, bf16[2,512,12,64]{1,3,2,0:T(8,128)(2,1)}, u32[]{:S(2)}) copy-start(bf16[2,512,12,64]{1,3,2,0:T(8,128)(2,1)} %get-tuple-element.400) | copy-start | bytes 4718596 | tf_op jit(solution)/shard_map/while
  383.6 6.4 %copy-start.4 = (bf16[2,512,12,64]{1,3,2,0:T(8,128)(2,1)S(1)}, bf16[2,512,12,64]{1,3,2,0:T(8,128)(2,1)}, u32[]{:S(2)}) copy-start(bf16[2,512,12,64]{1,3,2,0:T(8,128)(2,1)} %get-tuple-element.401) | copy-start | bytes 4718596 | tf_op jit(solution)/shard_map/while
  383.6 6.4 %copy-start.5 = (bf16[2,512,12,64]{1,3,2,0:T(8,128)(2,1)S(1)}, bf16[2,512,12,64]{1,3,2,0:T(8,128)(2,1)}, u32[]{:S(2)}) copy-start(bf16[2,512,12,64]{1,3,2,0:T(8,128)(2,1)} %get-tuple-element.400) | copy-start | bytes 4718596 | tf_op jit(solution)/shard_map/while
  450.3 1.9 copy-start.15
  453.8 4.3 copy-start.21
  455.4 4.6 copy-start.2
  455.4 5.9 copy-start.22
  458.1 6.3 %copy-start.13 = (bf16[1024,768]{1,0:T(8,128)(2,1)S(1)}, bf16[1024,768]{1,0:T(8,128)(2,1)}, u32[]{:S(2)}) copy-start(bf16[1024,768]{1,0:T(8,128)(2,1)} %copy.106) | copy-start | bytes 4718596
  458.1 6.3 %copy-start.19 = (f32[1024,8]{0,1:T(8,128)S(1)}, f32[1024,8]{0,1:T(8,128)}, u32[]{:S(2)}) copy-start(f32[1024,8]{0,1:T(8,128)} %copy-done.18) | copy-start | bytes 98308
  460.0 6.8 %copy-start.14 = (bf16[1024,768]{1,0:T(8,128)(2,1)S(1)}, bf16[1024,768]{1,0:T(8,128)(2,1)}, u32[]{:S(2)}) copy-start(bf16[1024,768]{1,0:T(8,128)(2,1)} %copy.105) | copy-start | bytes 4718596
  460.0 6.8 %copy-start.17 = (f32[1024,8]{0,1:T(8,128)S(1)}, f32[1024,8]{0,1:T(8,128)}, u32[]{:S(2)}) copy-start(f32[1024,8]{0,1:T(8,128)} %copy-done.16) | copy-start | bytes 98308
  470.5 4.8 copy-start.6
  475.3 6.6 %copy-start.8 = (f32[1024,768]{1,0:T(8,128)S(1)}, f32[1024,768]{1,0:T(8,128)}, u32[]{:S(2)}) copy-start(f32[1024,768]{1,0:T(8,128)} %fusion.160) | copy-start | bytes 9437188
  475.3 6.6 %copy-start.10 = (f32[1024,768]{1,0:T(8,128)S(1)}, f32[1024,768]{1,0:T(8,128)}, u32[]{:S(2)}) copy-start(f32[1024,768]{1,0:T(8,128)} %copy-done.9) | copy-start | bytes 9437188
  475.3 6.6 %copy-start.23 = (bf16[768,8]{0,1:T(8,128)(2,1)S(1)}, bf16[768,8]{0,1:T(8,128)(2,1)}, u32[]{:S(2)}) copy-start(bf16[768,8]{0,1:T(8,128)(2,1)} %param.42) | copy-start | bytes 36868
  475.3 6.6 %copy-start.28 = (f32[1024]{0:T(1024)S(1)}, f32[1024]{0:T(1024)}, u32[]{:S(2)}) copy-start(f32[1024]{0:T(1024)} %copy-done.27) | copy-start | bytes 12292
  (4 other events, 5.7 us)
Sparse Core Ops, SparseCore 0:
  11.0 61.0 all-gather.5
  74.9 52.4 all-gather.7
  130.3 63.7 all-gather.9
  196.9 62.4 all-gather.11
  475.4 122.3 all-reduce.3
